TPU v7x, 32 devices: a whole 2x2x4 slice. The times are simulated.
32 devices in a mesh: row: 8 (over y, x, core), col: 4 (over z).
Axes of the slice: x: 2, y: 2, z: 4, core: 2. Of those that a mesh axis runs over, the one named last changes fastest.
Arguments:
- skew_matrix: float32 [16384, 16384], P('row', 'col'), may hold values from -80 to 80, as said below
- first_reflector: float32 [16384, 128], P('row'), may hold values from -0.05625 to 0.05625
- first_factor: float32 [128, 128], replicated, may hold values from -0.6 to 1.5, as said below
- second_reflector: float32 [16384, 128], P('row'), may hold values from -0.05625 to 0.05625
- second_factor: float32 [128, 128], replicated, may hold values from -0.6 to 1.5, as said below
- vectors: float32 [16384, 4096], P('row', 'col'), may hold values from -6 to 6
Outputs:
- updated_matrix: float32 [16384, 16384], P('row', 'col')
- back_vectors: float32 [16384, 4096], P('row', 'col')
Inputs may be any that keep to these rules, and one draw needn't show every extreme that they name: skew_matrix is skew-symmetric: entry (i, j) equals minus entry (j, i) exactly. first_factor is upper triangular with a positive diagonal. second_factor is upper triangular with a positive diagonal.
All inputs are finite; a program needn't handle non-finite values.
Results may differ from a plain program's by a relative error of at most 0.000059.
Values sent between devices are 32-bit elements; how exact they have to be, the bound alone decides.
A program may use at most 192 MiB of HBM per device.

v0:
```python
import jax
import jax.numpy as jnp
from jax import lax
from jax.sharding import PartitionSpec as P


def multiply(left, right):
    return jnp.dot(left, right, precision=lax.Precision.HIGHEST, preferred_element_type=jnp.float32)


def inner_rows(left, right):
    return lax.dot_general(
        left,
        right,
        (((0,), (0,)), ((), ())),
        precision=lax.Precision.HIGHEST,
        preferred_element_type=jnp.float32,
    )


def transform(matrix, own_rows, col_rows, factor):
    partial_rows = multiply(matrix, col_rows)
    summed_rows = lax.psum(partial_rows, "col")
    partial_cols = inner_rows(matrix, own_rows)
    summed_cols = lax.psum(partial_cols, "row")
    plain_cols = -summed_cols
    gram = lax.psum(inner_rows(own_rows, summed_rows), "row")
    correction = multiply(multiply(factor.T, gram), factor)
    fixed_rows = multiply(summed_rows, factor) - 0.5 * multiply(own_rows, correction)
    fixed_cols = multiply(plain_cols, factor) - 0.5 * multiply(col_rows, correction)
    left = jnp.concatenate([own_rows, -fixed_rows], axis=1)
    right = jnp.concatenate([fixed_cols, col_rows], axis=1)
    update = lax.dot_general(
        left,
        right,
        (((1,), (1,)), ((), ())),
        precision=lax.Precision.HIGHEST,
        preferred_element_type=jnp.float32,
    )
    return matrix + update


def shards(skew_matrix, first_reflector, first_factor, second_reflector, second_factor, vectors):
    joined = jnp.concatenate([first_reflector, second_reflector], axis=1)
    correlation, projected = lax.psum(
        (inner_rows(first_reflector, second_reflector), inner_rows(joined, vectors)), "row"
    )
    top_right = -multiply(multiply(first_factor, correlation), second_factor)
    zeros_block = jnp.zeros_like(second_factor)
    compact = jnp.concatenate(
        [
            jnp.concatenate([first_factor, top_right], axis=1),
            jnp.concatenate([zeros_block, second_factor], axis=1),
        ],
        axis=0,
    )
    back_vectors = vectors - multiply(joined, multiply(compact, projected))
    cols_here = skew_matrix.shape[1]
    col_index = lax.axis_index("col")
    whole_first, whole_second = (
        lax.all_gather(first_reflector, "row", axis=0, tiled=True),
        lax.all_gather(second_reflector, "row", axis=0, tiled=True),
    )
    col_start = col_index * cols_here
    panel_first = lax.dynamic_slice_in_dim(whole_first, col_start, cols_here, 0)
    panel_second = lax.dynamic_slice_in_dim(whole_second, col_start, cols_here, 0)
    inner = transform(skew_matrix, first_reflector, panel_first, first_factor)
    updated_matrix = transform(inner, second_reflector, panel_second, second_factor)
    return (updated_matrix, back_vectors)


def solution(mesh):
    in_specs = (P("row", "col"), P("row", None), P(), P("row", None), P(), P("row", "col"))
    out_specs = (P("row", "col"), P("row", "col"))
    return jax.shard_map(shards, mesh=mesh, in_specs=in_specs, out_specs=out_specs, check_vma=False)
```

profile of v0, /device:TPU:0, one launch (start us, length us, event | category | flops | bytes accessed | tf_op | source)
XLA Modules:
  0.0 549.0 jit_solution(17140156105039725318)
XLA Ops:
  7.2 0.0 all-gather.3.cloned.1.call-start
  7.2 0.7 all-gather.3.cloned.1.call-update
  7.9 0.0 all-reduce.8.cloned.1.call-start
  7.9 58.9 %all-gather.3.cloned.1.call-done = f32[16384,128]{1,0:T(8,128)} async-done(((f32[2048,128]{1,0:T(8,128)}), f32[16384,128]{1,0:T(8,128)}) %all-gather.3.cloned.1.call-update) | async-done | bytes 8388624 | tf_op jit(solution)/shard_map/all_gather | solution.py:61
  66.9 1.7 constant_dynamic-slice_fusion.1
  68.6 0.0 copy-start.4
  68.6 1.3 copy-done.4
  69.9 41.9 %convolution_bitcast_fusion = f32[2048,128]{0,1:T(8,128)} fusion(f32[4096,128]{1,0:T(8,128)S(1)} %constant_dynamic-slice_fusion.1, f32[2048,4096]{1,0:T(8,128)} %param.6), kind=kOutput, calls=%fused_computation.13 | convolution fusion | flops 12884901888 | bytes 36700160 | tf_op jit(solution)/shard_map/dot_general | solution.py:8
  111.8 0.0 copy-start
  111.8 0.0 copy-start.1
  111.8 0.0 all-reduce.8.cloned.1.call-update
  111.8 0.0 all-gather.5.cloned.1.call-start
  111.9 0.7 all-gather.5.cloned.1.call-update
  112.6 0.0 all-reduce.14.cloned.1.call-start
  112.6 0.4 copy-done
  113.0 1.1 constant_dynamic-update-slice_fusion.1
  114.1 0.0 copy-done.1
  114.1 1.1 constant_dynamic-update-slice_fusion
  115.2 57.1 %fusion.39 = f32[4096,128]{1,0:T(8,128)} fusion(f32[2048,4096]{1,0:T(8,128)} %param.6, f32[2048,128]{1,0:T(8,128)S(1)} %copy-done), kind=kOutput, calls=%fused_computation.56 | convolution fusion | flops 12884901888 | bytes 36700160 | tf_op jit(solution)/shard_map/dot_general | solution.py:12
  172.3 0.0 all-reduce.8.cloned.1.call-done
  172.3 3.1 convolution_bitcast_fusion.2
  175.4 0.0 all-reduce.14.cloned.1.call-update
  175.4 0.0 all-reduce.10.cloned.1.call-start
  175.5 11.1 %fusion.47 = f32[256,1024]{1,0:T(8,128)} fusion(f32[2048,256]{1,0:T(8,128)} %constant_dynamic-update-slice_fusion, f32[2048,1024]{1,0:T(8,128)} %param.11), kind=kOutput, calls=%fused_computation.64 | convolution fusion | flops 6442450944 | bytes 11534336 | tf_op jit(solution)/shard_map/dot_general | solution.py:12
  186.5 2.4 fusion.45
  189.0 30.4 %all-gather.5.cloned.1.call-done = f32[16384,128]{1,0:T(8,128)} async-done(((f32[2048,128]{1,0:T(8,128)}), f32[16384,128]{1,0:T(8,128)}) %all-gather.5.cloned.1.call-update) | async-done | bytes 8388624 | tf_op jit(solution)/shard_map/all_gather | solution.py:62
  219.3 3.2 constant_dynamic-slice_fusion
  222.6 0.0 copy-done.8
  222.6 0.0 copy-done.6
  222.6 1.8 fusion.36
  224.4 60.9 %all-reduce.14.cloned.1.call-done = (f32[4096,128]{1,0:T(8,128)}, f32[128,128]{0,1:T(8,128)}) async-done(((f32[4096,128]{1,0:T(8,128)}, f32[128,128]{0,1:T(8,128)}), (f32[4096,128]{1,0:T(8,128)}, f32[128,128]{0,1:T(8,128)})) %all-reduce.14.cloned.1.call-update) | async-done | bytes 2162704 | tf_op jit(solution)/shard_map/psum | solution.py:25
  285.3 3.6 fusion.22
  288.9 0.0 copy-done.12
  288.9 0.2 fusion.37
  289.1 0.3 fusion.38
  289.4 0.0 copy-done.5
  289.4 1.9 fusion.1
  291.3 1.0 fusion.13
  292.3 0.0 copy-start.2
  292.3 33.7 %convolution_add_fusion.1 = f32[2048,4096]{1,0:T(8,128)} fusion(f32[2048,4096]{1,0:T(8,128)} %param.6, f32[4096,128]{1,0:T(8,128)S(1)} %copy-done.5, f32[4096,128]{1,0:T(8,128)S(1)} %fusion.1, f32[2048,128]{1,0:T(8,128)S(1)} %fusion.13, f32[2048,128]{1,0:T(8,128)S(1)} %copy-done), kind=kOutput, calls=%fused_computation.1 | convolution fusion | flops 25779765248 | bytes 73400320 | tf_op jit(solution)/shard_map/dot_general | solution.py:33
  325.9 0.0 copy-done.2
  325.9 30.9 %fusion.40 = f32[2048,128]{1,0:T(8,128)} fusion(f32[2048,4096]{1,0:T(8,128)} %convolution_add_fusion.1, f32[4096,128]{1,0:T(8,128)S(1)} %copy-done.2), kind=kOutput, calls=%fused_computation.57 | convolution fusion | flops 12884901888 | bytes 36700160 | tf_op jit(solution)/shard_map/dot_general | solution.py:8
  356.8 0.0 all-reduce.10.cloned.1.call-update
  356.8 0.0 all-reduce.12.cloned.1.call-start
  356.9 57.1 %fusion.44 = f32[4096,128]{1,0:T(8,128)} fusion(f32[2048,4096]{1,0:T(8,128)} %convolution_add_fusion.1, f32[2048,128]{1,0:T(8,128)S(1)} %copy-done.1), kind=kOutput, calls=%fused_computation.61 | convolution fusion | flops 12884901888 | bytes 36700160 | tf_op jit(solution)/shard_map/dot_general | solution.py:12
  414.0 0.0 all-reduce.10.cloned.1.call-done
  414.0 3.7 convolution_bitcast_fusion.1
  417.7 0.0 all-reduce.12.cloned.1.call-update
  417.7 1.2 copy-done.7
  418.9 0.0 copy-done.9
  418.9 1.0 fusion.41
  419.9 68.0 %all-reduce.12.cloned.1.call-done = (f32[4096,128]{1,0:T(8,128)}, f32[128,128]{0,1:T(8,128)}, f32[256,1024]{1,0:T(8,128)}, f32[128,128]{1,0:T(8,128)}) async-done(((f32[4096,128]{1,0:T(8,128)}, f32[128,128]{0,1:T(8,128)}, f32[256,1024]{1,0:T(8,128)}, f32[128,128]{1,0:T(8,128)}), (f32[4096,128]{1,0:T(8,128)}, f32[128,128]{0,1:T(8,128)}, f32[256,1024]{1,0:T(8,128)}, ...) | async-done | bytes 3276816 | tf_op jit(solution)/shard_map/psum | solution.py:25
  487.9 3.6 fusion.20
  491.4 0.0 copy-done.13
  491.5 0.2 fusion.42
  491.7 0.3 fusion.43
  492.0 0.0 copy-done.3
  492.0 1.9 fusion
  493.9 1.0 fusion.10
  494.9 0.3 fusion.46
  495.2 0.3 convolution_negate_fusion
  495.5 1.0 fusion.24
  496.5 12.2 %convolution_subtract_fusion = f32[2048,1024]{1,0:T(8,128)} fusion(f32[2048,1024]{1,0:T(8,128)} %param.11, f32[2048,256]{1,0:T(8,128)} %constant_dynamic-update-slice_fusion, f32[256,1024]{1,0:T(8,128)S(1)} %fusion.24), kind=kOutput, calls=%fused_computation.6 | convolution fusion | flops 6444548096 | bytes 19922944 | tf_op jit(solution)/shard_map/dot_general | solution.py:8
  508.7 33.0 %convolution_add_fusion = f32[2048,4096]{1,0:T(8,128)} fusion(f32[2048,4096]{1,0:T(8,128)} %convolution_add_fusion.1, f32[4096,128]{1,0:T(8,128)S(1)} %copy-done.3, f32[4096,128]{1,0:T(8,128)S(1)} %fusion, f32[2048,128]{1,0:T(8,128)S(1)} %fusion.10, f32[2048,128]{1,0:T(8,128)S(1)} %copy-done.1), kind=kOutput, calls=%fused_computation | convolution fusion | flops 25779765248 | bytes 73400320 | tf_op jit(solution)/shard_map/dot_general | solution.py:33
  (12 shorter events, 0.0 us)
Async XLA Ops:
  7.2 59.7 %all-gather.3.cloned.1.call-start = ((), (), s32[]{:S(2)}) async-start(), calls=%async_computation | async-start | bytes 9437184 | tf_op jit(solution)/shard_map/all_gather | solution.py:61
  7.9 164.4 %all-reduce.8.cloned.1.call-start = ((), (), s32[]{:S(2)}) async-start(), calls=%async_computation.1 | async-start | bytes 2097152 | tf_op jit(solution)/shard_map/psum | solution.py:23
  68.6 1.3 copy-start.4
  111.8 1.2 copy-start
  111.8 2.3 copy-start.1
  111.8 107.5 %all-gather.5.cloned.1.call-start = ((), (), s32[]{:S(2)}) async-start(), calls=%async_computation.2 | async-start | bytes 9437184 | tf_op jit(solution)/shard_map/all_gather | solution.py:62
  112.6 172.7 %all-reduce.14.cloned.1.call-start = ((), (), s32[]{:S(2)}) async-start(), calls=%async_computation.5 | async-start | bytes 4325376 | tf_op jit(solution)/shard_map/psum | solution.py:25
  175.4 238.6 %all-reduce.10.cloned.1.call-start = ((), (), s32[]{:S(2)}) async-start(), calls=%async_computation.3 | async-start | bytes 2097152 | tf_op jit(solution)/shard_map/psum | solution.py:23
  189.0 33.6 %copy-start.8 = (f32[128,128]{1,0:T(8,128)S(1)}, f32[128,128]{1,0:T(8,128)}, u32[]{:S(2)}) copy-start(f32[128,128]{1,0:T(8,128)} %param.8) | copy-start | bytes 196612
  219.3 3.2 copy-start.6
  285.3 3.6 copy-start.12
  285.3 4.1 copy-start.5
  292.3 33.7 %copy-start.2 = (f32[4096,128]{1,0:T(8,128)S(1)}, f32[4096,128]{1,0:T(8,128)}, u32[]{:S(2)}) copy-start(f32[4096,128]{1,0:T(8,128)} %constant_dynamic-slice_fusion) | copy-start | bytes 6291460
  356.8 131.0 %all-reduce.12.cloned.1.call-start = ((), (), s32[]{:S(2)}) async-start(), calls=%async_computation.4 | async-start | bytes 6553600 | tf_op jit(solution)/shard_map/psum | solution.py:25
  417.7 1.2 copy-start.7
  417.7 1.2 copy-start.9
  487.9 3.6 copy-start.13
  487.9 4.1 copy-start.3
  493.8 1.0 copy-start.11
  493.9 1.6 copy-start.10
Sparse Core Ops, SparseCore 0:
  9.9 56.9 all-gather.2
  112.0 51.8 all-reduce.7
  165.8 53.5 all-gather.4
  223.1 62.1 all-reduce.13
  357.0 51.0 all-reduce.9
  417.8 70.0 all-reduce.11
where the time goes:
time: 559 us; the launch traced here: 549 us
  matrix products  304 us (54%)
  waiting for transfers between devices  220 us (39%)
  between operations  14.8 us (3%)
  local copies, waits for them, and re-layouts  10 us (2%)
    dot_general x6, matrix products, inner_rows(): lax.dot_general(left, right, (((0,), (0,)), ((), ())), precision=lax.Prec...  134 us
    psum x2, waiting for transfers between devices, transform(): summed_cols = lax.psum(partial_cols, 'row')  129 us
    dot_general x18, matrix products, multiply(): jnp.dot(left, right, precision=lax.Precision.HIGHEST, preferred_element_t...  103 us
    dot_general x2, matrix products, transform(): lax.dot_general(left, right, (((1,), (1,)), ((), ())), precision=lax.Prec...  66.7 us
    all_gather x1, waiting for transfers between devices, shards(): lax.all_gather(first_reflector, 'row', axis=0, tiled=True)  58.9 us
    all_gather x1, waiting for transfers between devices, shards(): lax.all_gather(second_reflector, 'row', axis=0, tiled=True)  30.4 us
  transfers between devices with their start and end apart: 6, of which 4 were waited for; matrix products, arithmetic and copies ran while one was open for 25% of the time, Pallas kernels for 0%

commit v1 on v0

--- a/solution.py
+++ b/solution.py
@@ -22,7 +22,7 @@
     partial_rows = multiply(matrix, col_rows)
     summed_rows = lax.psum(partial_rows, "col")
     partial_cols = inner_rows(matrix, own_rows)
-    summed_cols = lax.psum(partial_cols, "row")
+    summed_cols = jax.lax.all_gather(partial_cols, axis_name="row").sum(axis=0)
     plain_cols = -summed_cols
     gram = lax.psum(inner_rows(own_rows, summed_rows), "row")
     correction = multiply(multiply(factor.T, gram), factor)

time: 559 us -> 712 us (1.27)
  waiting for transfers between devices: 220 us -> 351 us
  other arithmetic: 0 us -> 16.3 us
    all_gather x0 -> x2, waiting for transfers between devices: none -> 157 us  [transform(): summed_cols = jax.lax.all_gather(partial_cols, axis_name='row').sum(axis=0)]
    psum x2, waiting for transfers between devices: 0.04 us -> 88.8 us  [transform(): summed_rows = lax.psum(partial_rows, 'col')]
    psum x2, waiting for transfers between devices: 129 us -> 44.5 us  [transform(): gram = lax.psum(inner_rows(own_rows, summed_rows), 'row')]
    all_gather x1, waiting for transfers between devices: 30.4 us -> 0.01 us  [shards(): lax.all_gather(second_reflector, 'row', axis=0, tiled=True)]
    reduce_sum x0 -> x2, other arithmetic: none -> 16.3 us  [transform(): summed_cols = jax.lax.all_gather(partial_cols, axis_name='row').sum(axis=0)]
  transfers between devices with their start and end apart: 6 -> 8, of which waited for: 4 -> 6; matrix products, arithmetic and copies ran while one was open for 25% -> 23% of each run, Pallas kernels for 0% -> 0%
where the time goes in v1:
time: 712 us; the launch traced here: 701 us
  waiting for transfers between devices  351 us (49%)
  matrix products  309 us (43%)
  other arithmetic  16.3 us (2%)
  between operations  14.8 us (2%)
  local copies, waits for them, and re-layouts  9.27 us (1%)
    all_gather x2, waiting for transfers between devices, transform(): summed_cols = jax.lax.all_gather(partial_cols, axis_name='row').sum(axis=0)  157 us
    dot_general x6, matrix products, inner_rows(): lax.dot_general(left, right, (((0,), (0,)), ((), ())), precision=lax.Prec...  134 us
    dot_general x18, matrix products, multiply(): jnp.dot(left, right, precision=lax.Precision.HIGHEST, preferred_element_t...  109 us
    psum x2, waiting for transfers between devices, transform(): summed_rows = lax.psum(partial_rows, 'col')  88.8 us
    dot_general x2, matrix products, transform(): lax.dot_general(left, right, (((1,), (1,)), ((), ())), precision=lax.Prec...  66.7 us
    all_gather x1, waiting for transfers between devices, shards(): lax.all_gather(first_reflector, 'row', axis=0, tiled=True)  58.9 us
    psum x2, waiting for transfers between devices, transform(): gram = lax.psum(inner_rows(own_rows, summed_rows), 'row')  44.5 us
    reduce_sum x2, other arithmetic, transform(): summed_cols = jax.lax.all_gather(partial_cols, axis_name='row').sum(axis=0)  16.3 us
  transfers between devices with their start and end apart: 8, of which 6 were waited for; matrix products, arithmetic and copies ran while one was open for 23% of the time, Pallas kernels for 0%

profile of v1, /device:TPU:0, one launch (start us, length us, event | category | flops | bytes accessed | tf_op | source)
XLA Modules:
  0.0 701.4 jit_solution(14762369002562291343)
XLA Ops:
  7.2 0.0 all-gather.7.cloned.1.call-start
  7.2 0.7 all-gather.7.cloned.1.call-update
  7.9 0.0 all-reduce.7.cloned.1.call-start
  7.9 58.9 %all-gather.7.cloned.1.call-done = f32[16384,128]{1,0:T(8,128)} async-done(((f32[2048,128]{1,0:T(8,128)}), f32[16384,128]{1,0:T(8,128)}) %all-gather.7.cloned.1.call-update) | async-done | bytes 8388624 | tf_op jit(solution)/shard_map/all_gather | solution.py:61
  66.9 1.7 constant_dynamic-slice_fusion.1
  68.6 41.8 %convolution_bitcast_fusion = f32[2048,128]{0,1:T(8,128)} fusion(f32[4096,128]{1,0:T(8,128)S(1)} %constant_dynamic-slice_fusion.1, f32[2048,4096]{1,0:T(8,128)} %param.6), kind=kOutput, calls=%fused_computation.13 | convolution fusion | flops 12884901888 | bytes 36700160 | tf_op jit(solution)/shard_map/dot_general | solution.py:8
  110.4 0.0 copy-start
  110.4 0.0 all-reduce.7.cloned.1.call-update
  110.4 0.0 all-gather.9.cloned.1.call-start
  110.5 0.7 all-gather.9.cloned.1.call-update
  111.2 0.0 all-reduce.9.cloned.1.call-start
  111.2 51.3 %all-reduce.7.cloned.1.call-done = f32[2048,128]{0,1:T(8,128)} async-done(((f32[2048,128]{0,1:T(8,128)}), f32[2048,128]{0,1:T(8,128)}) %all-reduce.7.cloned.1.call-update) | async-done | bytes 1048592 | tf_op jit(solution)/shard_map/psum | solution.py:23
  162.5 0.0 copy-done
  162.5 3.0 convolution_bitcast_fusion.2
  165.5 0.0 all-reduce.9.cloned.1.call-update
  165.5 0.0 all-gather.11.cloned.1.call-start
  165.5 56.9 %fusion.39 = f32[4096,128]{1,0:T(8,128)} fusion(f32[2048,4096]{1,0:T(8,128)} %param.6, f32[2048,128]{1,0:T(8,128)S(1)} %copy-done), kind=kOutput, calls=%fused_computation.56 | convolution fusion | flops 12884901888 | bytes 36700160 | tf_op jit(solution)/shard_map/dot_general | solution.py:12
  222.4 0.0 all-gather.11.cloned.1.call-update
  222.4 0.0 all-reduce.11.cloned.1.call-start
  222.5 1.1 constant_dynamic-update-slice_fusion.1
  223.6 3.2 constant_dynamic-slice_fusion
  226.8 0.0 copy-done.9
  226.8 0.0 copy-done.7
  226.8 2.8 fusion.36
  229.6 44.5 %all-reduce.9.cloned.1.call-done = f32[128,128]{0,1:T(8,128)} async-done(((f32[128,128]{0,1:T(8,128)}), f32[128,128]{0,1:T(8,128)}) %all-reduce.9.cloned.1.call-update) | async-done | bytes 65552 | tf_op jit(solution)/shard_map/psum | solution.py:27
  274.1 1.0 fusion.37
  275.1 0.3 fusion.38
  275.4 3.2 fusion.13
  278.6 87.0 %all-gather.11.cloned.1.call-done = f32[32768,128]{1,0:T(8,128)} async-done(((f32[4096,128]{1,0:T(8,128)}), f32[32768,128]{1,0:T(8,128)}) %all-gather.11.cloned.1.call-update) | async-done | bytes 16777232 | tf_op jit(solution)/shard_map/all_gather | solution.py:25
  365.5 8.1 %reduce_sum.18 = f32[4096,128]{1,0:T(8,128)} reduce(f32[8,4096,128]{2,1,0:T(8,128)} %bitcast.66, f32[]{:T(128)} %constant.3.clone.1), dimensions={0}, to_apply=%region_2.0 | reduce | flops 3670016 | bytes 18874372 | tf_op jit(solution)/shard_map/reduce_sum | solution.py:25
  373.7 3.4 fusion.22
  377.1 0.0 copy-start.6
  377.1 1.9 fusion.1
  379.0 0.0 copy-done.6
  379.0 33.4 %convolution_add_fusion.1 = f32[2048,4096]{1,0:T(8,128)} fusion(f32[2048,4096]{1,0:T(8,128)} %param.6, f32[4096,128]{1,0:T(8,128)S(1)} %constant_dynamic-slice_fusion.1, f32[4096,128]{1,0:T(8,128)S(1)} %fusion.1, f32[2048,128]{1,0:T(8,128)S(1)} %copy-done.6, f32[2048,128]{1,0:T(8,128)S(1)} %copy-done), kind=kOutput, calls=%fused_computation.1 | convolution fusion | flops 25779765248 | bytes 73400320 | tf_op jit(solution)/shard_map/dot_general | solution.py:33
  412.4 31.0 %fusion.40 = f32[2048,128]{1,0:T(8,128)} fusion(f32[2048,4096]{1,0:T(8,128)} %convolution_add_fusion.1, f32[4096,128]{1,0:T(8,128)S(1)} %copy-done.2), kind=kOutput, calls=%fused_computation.57 | convolution fusion | flops 12884901888 | bytes 36700160 | tf_op jit(solution)/shard_map/dot_general | solution.py:8
  443.4 0.0 all-reduce.11.cloned.1.call-update
  443.4 0.4 all-reduce.13.cloned.1.call-start
  443.9 1.1 constant_dynamic-update-slice_fusion
  445.0 2.4 fusion.45
  447.4 10.5 %fusion.47 = f32[256,1024]{1,0:T(8,128)} fusion(f32[2048,256]{1,0:T(8,128)S(1)} %copy-done.4, f32[2048,1024]{1,0:T(8,128)} %param.11), kind=kOutput, calls=%fused_computation.64 | convolution fusion | flops 6442450944 | bytes 11534336 | tf_op jit(solution)/shard_map/dot_general | solution.py:12
  457.9 37.5 %all-reduce.11.cloned.1.call-done = f32[2048,128]{1,0:T(8,128)} async-done(((f32[2048,128]{1,0:T(8,128)}), f32[2048,128]{1,0:T(8,128)}) %all-reduce.11.cloned.1.call-update) | async-done | bytes 1048592 | tf_op jit(solution)/shard_map/psum | solution.py:23
  495.5 3.7 convolution_bitcast_fusion.1
  499.1 0.0 all-reduce.13.cloned.1.call-update
  499.2 0.0 all-gather.13.cloned.1.call-start
  499.2 57.1 %fusion.44 = f32[4096,128]{1,0:T(8,128)} fusion(f32[2048,4096]{1,0:T(8,128)} %convolution_add_fusion.1, f32[2048,128]{1,0:T(8,128)S(1)} %copy-done.1), kind=kOutput, calls=%fused_computation.61 | convolution fusion | flops 12884901888 | bytes 36700160 | tf_op jit(solution)/shard_map/dot_general | solution.py:12
  556.3 0.0 copy-start.10
  556.3 0.0 all-gather.13.cloned.1.call-update
  556.4 1.2 copy-done.8
  557.5 1.0 fusion.41
  558.5 0.0 all-reduce.13.cloned.1.call-done
  558.5 1.0 fusion.42
  559.6 0.3 fusion.43
  559.9 1.1 fusion.46
  561.0 0.3 convolution_negate_fusion
  561.3 2.2 fusion.24
  563.6 1.0 fusion.10
  564.6 1.0 copy-done.5
  565.5 11.4 %convolution_subtract_fusion = f32[2048,1024]{1,0:T(8,128)} fusion(f32[2048,1024]{1,0:T(8,128)} %param.11, f32[2048,256]{1,0:T(8,128)S(1)} %copy-done.5, f32[256,1024]{1,0:T(8,128)S(1)} %fusion.24), kind=kOutput, calls=%fused_computation.6 | convolution fusion | flops 6444548096 | bytes 19922944 | tf_op jit(solution)/shard_map/dot_general | solution.py:8
  576.9 70.3 %all-gather.13.cloned.1.call-done = f32[32768,128]{1,0:T(8,128)} async-done(((f32[4096,128]{1,0:T(8,128)}), f32[32768,128]{1,0:T(8,128)}) %all-gather.13.cloned.1.call-update) | async-done | bytes 16777232 | tf_op jit(solution)/shard_map/all_gather | solution.py:25
  647.2 8.1 %reduce_sum.19 = f32[4096,128]{1,0:T(8,128)} reduce(f32[8,4096,128]{2,1,0:T(8,128)} %bitcast.65, f32[]{:T(128)} %constant.3.clone.1), dimensions={0}, to_apply=%region_5.0 | reduce | flops 3670016 | bytes 18874372 | tf_op jit(solution)/shard_map/reduce_sum | solution.py:25
  655.3 3.6 fusion.20
  658.9 1.9 fusion
  660.8 33.3 %convolution_add_fusion = f32[2048,4096]{1,0:T(8,128)} fusion(f32[2048,4096]{1,0:T(8,128)} %convolution_add_fusion.1, f32[4096,128]{1,0:T(8,128)S(1)} %copy-done.3, f32[4096,128]{1,0:T(8,128)S(1)} %fusion, f32[2048,128]{1,0:T(8,128)S(1)} %fusion.10, f32[2048,128]{1,0:T(8,128)S(1)} %copy-done.1), kind=kOutput, calls=%fused_computation | convolution fusion | flops 25779765248 | bytes 73400320 | tf_op jit(solution)/shard_map/dot_general | solution.py:33
  (14 shorter events, 0.0 us)
Async XLA Ops:
  7.2 59.7 %all-gather.7.cloned.1.call-start = ((), (), s32[]{:S(2)}) async-start(), calls=%async_computation | async-start | bytes 9437184 | tf_op jit(solution)/shard_map/all_gather | solution.py:61
  7.9 154.6 %all-reduce.7.cloned.1.call-start = ((), (), s32[]{:S(2)}) async-start(), calls=%async_computation.1 | async-start | bytes 2097152 | tf_op jit(solution)/shard_map/psum | solution.py:23
  110.4 52.1 %copy-start = (f32[2048,128]{1,0:T(8,128)S(1)}, f32[2048,128]{1,0:T(8,128)}, u32[]{:S(2)}) copy-start(f32[2048,128]{1,0:T(8,128)} %param.7) | copy-start | bytes 3145732
  110.4 113.1 %all-gather.9.cloned.1.call-start = ((), (), s32[]{:S(2)}) async-start(), calls=%async_computation.3 | async-start | bytes 9437184 | tf_op jit(solution)/shard_map/all_gather | solution.py:62
  111.2 162.9 %all-reduce.9.cloned.1.call-start = ((), (), s32[]{:S(2)}) async-start(), calls=%async_computation.2 | async-start | bytes 131072 | tf_op jit(solution)/shard_map/psum | solution.py:27
  165.5 200.1 %all-gather.11.cloned.1.call-start = ((), (), s32[]{:S(2)}) async-start(), calls=%async_computation.5 | async-start | bytes 18874368 | tf_op jit(solution)/shard_map/all_gather | solution.py:25
  222.4 273.0 %all-reduce.11.cloned.1.call-start = ((), (), s32[]{:S(2)}) async-start(), calls=%async_computation.4 | async-start | bytes 2097152 | tf_op jit(solution)/shard_map/psum | solution.py:23
  223.6 3.2 copy-start.9
  223.6 3.2 copy-start.7
  377.1 1.9 copy-start.6
  379.0 33.4 %copy-start.2 = (f32[4096,128]{1,0:T(8,128)S(1)}, f32[4096,128]{1,0:T(8,128)}, u32[]{:S(2)}) copy-start(f32[4096,128]{1,0:T(8,128)} %constant_dynamic-slice_fusion) | copy-start | bytes 6291460
  412.4 31.4 %copy-start.1 = (f32[2048,128]{1,0:T(8,128)S(1)}, f32[2048,128]{1,0:T(8,128)}, u32[]{:S(2)}) copy-start(f32[2048,128]{1,0:T(8,128)} %param.9) | copy-start | bytes 3145732
  443.4 115.1 %all-reduce.13.cloned.1.call-start = ((), (), s32[]{:S(2)}) async-start(), calls=%async_computation.7 | async-start | bytes 2359296 | tf_op jit(solution)/shard_map/psum | solution.py:27
  445.0 2.4 copy-start.4
  499.2 148.0 %all-gather.13.cloned.1.call-start = ((), (), s32[]{:S(2)}) async-start(), calls=%async_computation.6 | async-start | bytes 18874368 | tf_op jit(solution)/shard_map/all_gather | solution.py:25
  556.3 1.2 copy-start.8
  556.3 1.2 copy-start.10
  563.6 1.9 copy-start.5
  655.3 3.6 copy-start.3
Sparse Core Ops, SparseCore 0:
  9.9 56.9 all-gather.6
  110.6 51.8 all-reduce.6
  164.4 53.5 all-gather.8
  220.8 53.1 all-reduce.8
  276.4 89.1 all-gather.10
  443.5 51.8 all-reduce.10
  499.5 56.7 all-reduce.12
  558.2 88.9 all-gather.12
